TPU v7x, 32 devices: a whole 2x2x4 slice. The times are simulated.
32 devices in a mesh: dp: 8 (over z, y), ctx: 4 (over x, core).
Axes of the slice: x: 2, y: 2, z: 4, core: 2. Of those that a mesh axis runs over, the one named last changes fastest.
Arguments:
- tokens: bfloat16 [8, 1024, 2048], P('dp', 'ctx'), may hold values from -6 to 6
- cotangent: bfloat16 [8, 1024, 2048], P('dp', 'ctx'), may hold values from -6 to 6
- domain_ids: int32 [8], P('dp'), may hold values from 0 to 31
- domain_counts: int32 [32], replicated, may hold values from 1024 to 4096
- domain_numer: int32 [32], replicated, may hold values from 1 to 8
- domain_denom: int32 [32], replicated, may hold values from 1 to 8
- attention_gain: bfloat16 [2048], replicated, may hold values from 0.5 to 1.5
- query_gain: bfloat16 [128], replicated, may hold values from 0.796875 to 1.796875
- key_gain: bfloat16 [128], replicated, may hold values from 0.796875 to 1.796875
- query_proj: bfloat16 [2048, 2048], P('dp', 'ctx'), may hold values from -0.125 to 0.125
- key_proj: bfloat16 [2048, 1024], P('dp', 'ctx'), may hold values from -0.125 to 0.125
- value_proj: bfloat16 [2048, 1024], P('dp', 'ctx'), may hold values from -0.125 to 0.125
- gating_proj: bfloat16 [2048, 2048], P('dp', 'ctx'), may hold values from -0.125 to 0.125
- output_proj: bfloat16 [2048, 2048], P('ctx', 'dp'), may hold values from -1 to 1
- swiglu_gain: bfloat16 [2048], replicated, may hold values from 0.5 to 1.5
- swiglu_gate: bfloat16 [2048, 6144], P('dp', 'ctx'), may hold values from -0.125 to 0.125
- swiglu_up: bfloat16 [2048, 6144], P('dp', 'ctx'), may hold values from -0.125 to 0.125
- swiglu_down: bfloat16 [6144, 2048], P('ctx', 'dp'), may hold values from -0.109375 to 0.109375
Outputs:
- layer_out: bfloat16 [8, 1024, 2048], P('dp', 'ctx')
- input_grad: bfloat16 [8, 1024, 2048], P('dp', 'ctx')
- attention_gain_grad: float32 [2048], replicated
- query_gain_grad: float32 [128], replicated
- key_gain_grad: float32 [128], replicated
- query_proj_grad: float32 [2048, 2048], P('dp', 'ctx')
- key_proj_grad: float32 [2048, 1024], P('dp', 'ctx')
- value_proj_grad: float32 [2048, 1024], P('dp', 'ctx')
- gating_proj_grad: float32 [2048, 2048], P('dp', 'ctx')
- output_proj_grad: float32 [2048, 2048], P('ctx', 'dp')
- swiglu_gain_grad: float32 [2048], replicated
- swiglu_gate_grad: float32 [2048, 6144], P('dp', 'ctx')
- swiglu_up_grad: float32 [2048, 6144], P('dp', 'ctx')
- swiglu_down_grad: float32 [6144, 2048], P('ctx', 'dp')
All inputs are finite; a program needn't handle non-finite values.
Results may differ from a plain program's by a relative error of at most 0.019.
Values may be sent and summed in bfloat16 or wider, within the bound.
A program may use at most 192 MiB of HBM per device.

v0:
```python
import jax
import jax.numpy as jnp
from jax import lax
from jax.sharding import PartitionSpec as P

LENGTH = 1024
EPSILON = 1e-06
ROPE_BASE = 1000000.0


def matmul_f32(left, right):
    return jnp.dot(left, right, preferred_element_type=jnp.float32)


def matmul_tn(left, right):
    return lax.dot_general(
        left, right, (((0,), (0,)), ((), ())), preferred_element_type=jnp.float32
    )


def matmul_nt(left, right):
    return lax.dot_general(
        left, right, (((1,), (1,)), ((), ())), preferred_element_type=jnp.float32
    )


def rope_tables(positions, head_width):
    halfway = head_width // 2
    inverse = 1.0 / ROPE_BASE ** (jnp.arange(halfway, dtype=jnp.float32) * (2.0 / head_width))
    angles = positions.astype(jnp.float32)[:, None] * inverse[None, :]
    return (jnp.cos(angles), jnp.sin(angles))


def rotate(tensor, cosine, sine):
    halfway = tensor.shape[-1] // 2
    first_half = tensor[..., :halfway]
    second_half = tensor[..., halfway:]
    return jnp.concatenate(
        [first_half * cosine - second_half * sine, second_half * cosine + first_half * sine], -1
    )


def unrotate(grads_in, cosine, sine):
    halfway = grads_in.shape[-1] // 2
    first_half = grads_in[..., :halfway]
    second_half = grads_in[..., halfway:]
    return jnp.concatenate(
        [first_half * cosine + second_half * sine, second_half * cosine - first_half * sine], -1
    )


def norm_back(grads_in, values_in, inverse, gain_vec):
    scaled = grads_in * gain_vec
    return inverse * scaled - values_in * (inverse * inverse * inverse) * jnp.mean(
        scaled * values_in, -1, keepdims=True
    )


def attention_weights(query_proj, key_proj, value_proj, gating_proj, output_proj):
    return (
        lax.all_gather(query_proj, "dp", axis=0, tiled=True),
        lax.all_gather(key_proj, "dp", axis=0, tiled=True),
        lax.all_gather(value_proj, "dp", axis=0, tiled=True),
        lax.all_gather(gating_proj, "dp", axis=0, tiled=True),
        lax.all_gather(output_proj, "dp", axis=1, tiled=True),
    )


def swiglu_weights(swiglu_gate, swiglu_up, swiglu_down):
    return (
        lax.all_gather(swiglu_gate, "dp", axis=0, tiled=True),
        lax.all_gather(swiglu_up, "dp", axis=0, tiled=True),
        lax.all_gather(swiglu_down, "dp", axis=1, tiled=True),
    )


def softmax_forward(seq_items, causal):
    queries, keys_seq, values_seq = seq_items
    scaling = queries.shape[-1] ** (-0.5)
    scores = (
        jnp.einsum("qgjd,kgd->gjqk", queries, keys_seq, preferred_element_type=jnp.float32)
        * scaling
    )
    scores = jnp.where(causal, scores, -1e30)
    highest = jnp.max(scores, -1, keepdims=True)
    exp_vals = jnp.exp(scores - highest)
    row_totals = jnp.sum(exp_vals, -1, keepdims=True)
    attn_probs = (exp_vals / row_totals).astype(jnp.bfloat16)
    attended = jnp.einsum(
        "gjqk,kgd->qgjd", attn_probs, values_seq, preferred_element_type=jnp.float32
    )
    return (attended, highest[..., 0] + jnp.log(row_totals[..., 0]))


def softmax_backward(seq_items, causal):
    queries, keys_seq, values_seq, log_total, upstream = seq_items
    scaling = queries.shape[-1] ** (-0.5)
    scores = (
        jnp.einsum("qgjd,kgd->gjqk", queries, keys_seq, preferred_element_type=jnp.float32)
        * scaling
    )
    scores = jnp.where(causal, scores, -1e30)
    attn_probs = jnp.exp(scores - log_total[..., None])
    dprobs = jnp.einsum("qgjd,kgd->gjqk", upstream, values_seq, preferred_element_type=jnp.float32)
    centre = jnp.sum(dprobs * attn_probs, -1, keepdims=True)
    dscores = (attn_probs * (dprobs - centre)).astype(jnp.bfloat16)
    dqueries = (
        jnp.einsum("gjqk,kgd->qgjd", dscores, keys_seq, preferred_element_type=jnp.float32)
        * scaling
    )
    key_grads = (
        jnp.einsum("gjqk,qgjd->kgd", dscores, queries, preferred_element_type=jnp.float32) * scaling
    )
    value_grads = jnp.einsum(
        "gjqk,qgjd->kgd",
        attn_probs.astype(jnp.bfloat16),
        upstream,
        preferred_element_type=jnp.float32,
    )
    key_rows = key_grads.shape[0]
    return (dqueries, key_grads.reshape(key_rows, -1), value_grads.reshape(key_rows, -1))


def per_device(
    tokens,
    cotangent,
    domain_ids,
    domain_counts,
    domain_numer,
    domain_denom,
    attention_gain,
    query_gain,
    key_gain,
    query_proj,
    key_proj,
    value_proj,
    gating_proj,
    output_proj,
    swiglu_gain,
    swiglu_gate,
    swiglu_up,
    swiglu_down,
):
    seq_count, local_len, model_width = tokens.shape
    full_len = local_len * lax.axis_size("ctx")
    local_rows = seq_count * local_len
    all_rows = seq_count * full_len
    head_dim = query_gain.shape[0]
    local_heads = query_proj.shape[1] // head_dim
    local_kv = key_proj.shape[1] // head_dim
    group_size = local_heads // local_kv
    positions = jnp.arange(full_len, dtype=jnp.int32)
    causal = positions[:, None] >= positions[None, :]
    cosine, sine = rope_tables(positions, head_dim)
    cos_rows = cosine[:, None, :]
    sin_rows = sine[:, None, :]
    inputs = tokens.reshape(local_rows, model_width).astype(jnp.float32)
    inverse_in = lax.rsqrt(jnp.mean(inputs * inputs, -1, keepdims=True) + EPSILON)
    gain_in = attention_gain.astype(jnp.float32)
    normed = (inputs * inverse_in * gain_in).astype(jnp.bfloat16)
    normed_all = lax.all_gather(
        normed.reshape(seq_count, local_len, model_width), "ctx", axis=1, tiled=True
    ).reshape(all_rows, model_width)
    attn_full = attention_weights(query_proj, key_proj, value_proj, gating_proj, output_proj)
    query_raw = matmul_f32(normed_all, attn_full[0]).reshape(
        seq_count, full_len, local_heads, head_dim
    )
    key_raw = matmul_f32(normed_all, attn_full[1]).reshape(seq_count, full_len, local_kv, head_dim)
    value_low = (
        matmul_f32(normed_all, attn_full[2])
        .astype(jnp.bfloat16)
        .reshape(seq_count, full_len, local_kv, head_dim)
    )
    gate_pre = matmul_f32(normed_all, attn_full[3])
    query_scale = query_gain.astype(jnp.float32)
    key_scale = key_gain.astype(jnp.float32)
    query_inv = lax.rsqrt(jnp.mean(query_raw * query_raw, -1, keepdims=True) + EPSILON)
    key_inv = lax.rsqrt(jnp.mean(key_raw * key_raw, -1, keepdims=True) + EPSILON)
    query_low = rotate(query_raw * query_inv * query_scale, cos_rows, sin_rows).astype(jnp.bfloat16)
    key_low = rotate(key_raw * key_inv * key_scale, cos_rows, sin_rows).astype(jnp.bfloat16)
    query_groups = query_low.reshape(seq_count, full_len, local_kv, group_size, head_dim)
    attended, log_total = lax.map(
        lambda seq_items: softmax_forward(seq_items, causal), (query_groups, key_low, value_low)
    )
    attended = attended.reshape(all_rows, local_heads * head_dim)
    gate_sig = jax.nn.sigmoid(gate_pre)
    mixed = (attended * gate_sig).astype(jnp.bfloat16)
    branch_part = matmul_f32(mixed, attn_full[4]).reshape(seq_count, full_len, model_width)
    branch = lax.psum_scatter(branch_part, "ctx", scatter_dimension=1, tiled=True).reshape(
        local_rows, model_width
    )
    hidden = inputs + branch
    inverse_mid = lax.rsqrt(jnp.mean(hidden * hidden, -1, keepdims=True) + EPSILON)
    gain_mid = swiglu_gain.astype(jnp.float32)
    normed_mid = (hidden * inverse_mid * gain_mid).astype(jnp.bfloat16)
    normed_mid_all = lax.all_gather(
        normed_mid.reshape(seq_count, local_len, model_width), "ctx", axis=1, tiled=True
    ).reshape(all_rows, model_width)
    swiglu_full = swiglu_weights(swiglu_gate, swiglu_up, swiglu_down)
    gate_ff = matmul_f32(normed_mid_all, swiglu_full[0])
    up_val = matmul_f32(normed_mid_all, swiglu_full[1])
    gate_sigma = jax.nn.sigmoid(gate_ff)
    silu_val = gate_ff * gate_sigma
    activation = (silu_val * up_val).astype(jnp.bfloat16)
    down_part = matmul_f32(activation, swiglu_full[2]).reshape(seq_count, full_len, model_width)
    ffn_branch = (
        lax.psum_scatter(down_part.astype(jnp.bfloat16), "ctx", scatter_dimension=1, tiled=True)
        .astype(jnp.float32)
        .reshape(local_rows, model_width)
    )
    layer_out = (hidden + ffn_branch).astype(jnp.bfloat16)
    domain_table = (
        domain_ids[:, None] == jnp.arange(domain_counts.shape[0], dtype=jnp.int32)[None, :]
    ).astype(jnp.float32)
    ratio = (
        domain_numer.astype(jnp.float32)
        / domain_denom.astype(jnp.float32)
        * LENGTH
        / domain_counts.astype(jnp.float32)
    )
    factor = jnp.sum(domain_table * ratio[None, :], 1)
    upstream = (cotangent.astype(jnp.float32) * factor[:, None, None]).reshape(
        local_rows, model_width
    )
    swiglu_back = swiglu_weights(swiglu_gate, swiglu_up, swiglu_down)
    out_low = upstream.astype(jnp.bfloat16)
    out_all = lax.all_gather(
        out_low.reshape(seq_count, local_len, model_width), "ctx", axis=1, tiled=True
    ).reshape(all_rows, model_width)
    dactivation = matmul_nt(out_all, swiglu_back[2])
    dgate_low = (dactivation * up_val * gate_sigma * (1.0 + gate_ff * (1.0 - gate_sigma))).astype(
        jnp.bfloat16
    )
    dup_low = (dactivation * silu_val).astype(jnp.bfloat16)
    grad_down = matmul_tn(activation, out_all)
    grad_gate = matmul_tn(normed_mid_all, dgate_low)
    grad_up = matmul_tn(normed_mid_all, dup_low)
    dmid_part = matmul_nt(dgate_low, swiglu_back[0]) + matmul_nt(dup_low, swiglu_back[1])
    dnormed_mid = lax.psum_scatter(
        dmid_part.reshape(seq_count, full_len, model_width), "ctx", scatter_dimension=1, tiled=True
    ).reshape(local_rows, model_width)
    grad_gain_mid = jnp.sum(dnormed_mid * hidden * inverse_mid, 0)
    dhidden = upstream + norm_back(dnormed_mid, hidden, inverse_mid, gain_mid)
    swiglu_grads = (
        lax.psum_scatter(
            grad_gate.astype(jnp.bfloat16), "dp", scatter_dimension=0, tiled=True
        ).astype(jnp.float32),
        lax.psum_scatter(
            grad_up.astype(jnp.bfloat16), "dp", scatter_dimension=0, tiled=True
        ).astype(jnp.float32),
        lax.psum_scatter(
            grad_down.astype(jnp.bfloat16), "dp", scatter_dimension=1, tiled=True
        ).astype(jnp.float32),
    )
    attn_back = attention_weights(query_proj, key_proj, value_proj, gating_proj, output_proj)
    dbranch_low = dhidden.astype(jnp.bfloat16)
    dbranch_all = lax.all_gather(
        dbranch_low.reshape(seq_count, local_len, model_width), "ctx", axis=1, tiled=True
    ).reshape(all_rows, model_width)
    grad_output = matmul_tn(mixed, dbranch_all)
    dmixed = matmul_nt(dbranch_all, attn_back[4])
    dattended_low = (dmixed * gate_sig).astype(jnp.bfloat16)
    dgating_low = (dmixed * attended * gate_sig * (1.0 - gate_sig)).astype(jnp.bfloat16)
    upstream_heads = dattended_low.reshape(seq_count, full_len, local_kv, group_size, head_dim)
    dquery_rot, dkey_rot, dvalue_sum = lax.map(
        lambda seq_items: softmax_backward(seq_items, causal),
        (query_groups, key_low, value_low, log_total, upstream_heads),
    )
    dvalue_low = dvalue_sum.reshape(all_rows, local_kv * head_dim).astype(jnp.bfloat16)
    dquery_normed = unrotate(
        dquery_rot.reshape(seq_count, full_len, local_heads, head_dim), cos_rows, sin_rows
    )
    dkey_normed = unrotate(
        dkey_rot.reshape(seq_count, full_len, local_kv, head_dim), cos_rows, sin_rows
    )
    grad_query_gain = jnp.sum(dquery_normed * query_raw * query_inv, (0, 1, 2))
    grad_key_gain = jnp.sum(dkey_normed * key_raw * key_inv, (0, 1, 2))
    dquery_low = (
        norm_back(dquery_normed, query_raw, query_inv, query_scale)
        .reshape(all_rows, -1)
        .astype(jnp.bfloat16)
    )
    dkey_low = (
        norm_back(dkey_normed, key_raw, key_inv, key_scale)
        .reshape(all_rows, -1)
        .astype(jnp.bfloat16)
    )
    dnormed_part = (
        matmul_nt(dquery_low, attn_back[0])
        + matmul_nt(dkey_low, attn_back[1])
        + matmul_nt(dvalue_low, attn_back[2])
        + matmul_nt(dgating_low, attn_back[3])
    )
    dnormed = (
        lax.psum_scatter(
            dnormed_part.reshape(seq_count, full_len, model_width).astype(jnp.bfloat16),
            "ctx",
            scatter_dimension=1,
            tiled=True,
        )
        .astype(jnp.float32)
        .reshape(local_rows, model_width)
    )
    grad_gain_in = jnp.sum(dnormed * inputs * inverse_in, 0)
    input_grad = (dhidden + norm_back(dnormed, inputs, inverse_in, gain_in)).astype(jnp.bfloat16)
    grad_query = matmul_tn(normed_all, dquery_low)
    grad_key = matmul_tn(normed_all, dkey_low)
    grad_value = matmul_tn(normed_all, dvalue_low)
    grad_gating = matmul_tn(normed_all, dgating_low)
    attention_grads = (
        lax.psum_scatter(
            grad_query.astype(jnp.bfloat16), "dp", scatter_dimension=0, tiled=True
        ).astype(jnp.float32),
        lax.psum_scatter(
            grad_key.astype(jnp.bfloat16), "dp", scatter_dimension=0, tiled=True
        ).astype(jnp.float32),
        lax.psum_scatter(
            grad_value.astype(jnp.bfloat16), "dp", scatter_dimension=0, tiled=True
        ).astype(jnp.float32),
        lax.psum_scatter(
            grad_gating.astype(jnp.bfloat16), "dp", scatter_dimension=0, tiled=True
        ).astype(jnp.float32),
        lax.psum_scatter(
            grad_output.astype(jnp.bfloat16), "dp", scatter_dimension=1, tiled=True
        ).astype(jnp.float32),
    )
    gain_grads = lax.psum(
        (grad_gain_in, grad_gain_mid, grad_query_gain, grad_key_gain), ("dp", "ctx")
    )
    return (
        layer_out.reshape(seq_count, local_len, model_width),
        input_grad.reshape(seq_count, local_len, model_width),
        gain_grads[0],
        gain_grads[2],
        gain_grads[3],
        attention_grads[0],
        attention_grads[1],
        attention_grads[2],
        attention_grads[3],
        attention_grads[4],
        gain_grads[1],
        swiglu_grads[0],
        swiglu_grads[1],
        swiglu_grads[2],
    )


def solution(mesh):
    return jax.shard_map(
        per_device,
        mesh=mesh,
        in_specs=(
            P("dp", "ctx", None),
            P("dp", "ctx", None),
            P("dp"),
            P(),
            P(),
            P(),
            P(),
            P(),
            P(),
            P("dp", "ctx"),
            P("dp", "ctx"),
            P("dp", "ctx"),
            P("dp", "ctx"),
            P("ctx", "dp"),
            P(),
            P("dp", "ctx"),
            P("dp", "ctx"),
            P("ctx", "dp"),
        ),
        out_specs=(
            P("dp", "ctx", None),
            P("dp", "ctx", None),
            P(),
            P(),
            P(),
            P("dp", "ctx"),
            P("dp", "ctx"),
            P("dp", "ctx"),
            P("dp", "ctx"),
            P("ctx", "dp"),
            P(),
            P("dp", "ctx"),
            P("dp", "ctx"),
            P("ctx", "dp"),
        ),
        check_vma=False,
    )
```

profile of v0, /device:TPU:0, one launch (start us, length us, event | category | flops | bytes accessed | tf_op | source)
XLA Modules:
  0.0 1734.3 jit_solution(1612069383806065240)
XLA Ops:
  18.6 34.5 %all-gather.17.cloned.1.call-done = bf16[2048,256]{1,0:T(8,128)(2,1)} async-done(((bf16[256,256]{1,0:T(8,128)(2,1)}), bf16[2048,256]{1,0:T(8,128)(2,1)}) %all-gather.17.cloned.1.call-update) | async-done | bytes 1048592 | tf_op jit(solution)/shard_map/all_gather | solution.py:62
  53.1 35.4 %all-gather.13.cloned.1.call-done = bf16[1,1024,2048]{2,1,0:T(8,128)(2,1)} async-done(((bf16[1,256,2048]{2,1,0:T(8,128)(2,1)}), bf16[1,1024,2048]{2,1,0:T(8,128)(2,1)}) %all-gather.13.cloned.1.call-update) | async-done | bytes 4194320 | tf_op jit(solution)/shard_map/all_gather | solution.py:161
  93.4 46.5 %all-gather.19.cloned.1.call-done = bf16[2048,512]{1,0:T(8,128)(2,1)} async-done(((bf16[256,512]{1,0:T(8,128)(2,1)}), bf16[2048,512]{1,0:T(8,128)(2,1)}) %all-gather.19.cloned.1.call-update) | async-done | bytes 2097168 | tf_op jit(solution)/shard_map/all_gather | solution.py:61
  153.7 8.3 fusion.106
  162.1 18.5 %all-gather.15.cloned.1.call-done = bf16[2048,256]{1,0:T(8,128)(2,1)} async-done(((bf16[256,256]{1,0:T(8,128)(2,1)}), bf16[2048,256]{1,0:T(8,128)(2,1)}) %all-gather.15.cloned.1.call-update) | async-done | bytes 1048592 | tf_op jit(solution)/shard_map/all_gather | solution.py:63
  184.4 8.4 fusion.3
  192.9 7.5 fusion.8
  200.4 30.3 %all-gather.21.cloned.1.call-done = bf16[2048,512]{1,0:T(8,128)(2,1)} async-done(((bf16[256,512]{1,0:T(8,128)(2,1)}), bf16[2048,512]{1,0:T(8,128)(2,1)}) %all-gather.21.cloned.1.call-update) | async-done | bytes 2097168 | tf_op jit(solution)/shard_map/all_gather | solution.py:64
  230.7 6.9 fusion.74
  237.5 44.6 %all-gather.23.cloned.1.call-done = bf16[512,2048]{1,0:T(8,128)(2,1)} async-done(((bf16[512,256]{1,0:T(8,128)(2,1)}), bf16[512,2048]{1,0:T(8,128)(2,1)}) %all-gather.23.cloned.1.call-update) | async-done | bytes 2097168 | tf_op jit(solution)/shard_map/all_gather | solution.py:65
  282.1 7.3 convolution_bitcast_fusion
  290.3 69.2 %reduce-scatter.13.cloned.1.call-done = f32[1,256,2048]{2,1,0:T(8,128)} async-done(((f32[1,1024,2048]{2,1,0:T(8,128)}), f32[1,256,2048]{2,1,0:T(8,128)}) %reduce-scatter.13.cloned.1.call-update) | async-done | bytes 2097168 | tf_op jit(solution)/shard_map/reduce_scatter | solution.py:189
  368.7 92.3 %all-gather.29.cloned.1.call-done = bf16[2048,1536]{1,0:T(8,128)(2,1)} async-done(((bf16[256,1536]{1,0:T(8,128)(2,1)}), bf16[2048,1536]{1,0:T(8,128)(2,1)}) %all-gather.29.cloned.1.call-update) | async-done | bytes 6291472 | tf_op jit(solution)/shard_map/all_gather | solution.py:72
  461.0 34.9 %all-gather.25.cloned.1.call-done = bf16[1,1024,2048]{2,1,0:T(8,128)(2,1)} async-done(((bf16[1,256,2048]{2,1,0:T(8,128)(2,1)}), bf16[1,1024,2048]{2,1,0:T(8,128)(2,1)}) %all-gather.25.cloned.1.call-update) | async-done | bytes 4194320 | tf_op jit(solution)/shard_map/all_gather | solution.py:196
  495.9 11.7 fusion.19
  507.7 89.6 %all-gather.27.cloned.1.call-done = bf16[2048,1536]{1,0:T(8,128)(2,1)} async-done(((bf16[256,1536]{1,0:T(8,128)(2,1)}), bf16[2048,1536]{1,0:T(8,128)(2,1)}) %all-gather.27.cloned.1.call-update) | async-done | bytes 6291472 | tf_op jit(solution)/shard_map/all_gather | solution.py:71
  597.3 11.7 fusion.21
  609.0 23.2 %all-gather.33.cloned.1.call-done = bf16[1,1024,2048]{2,1,0:T(8,128)(2,1)} async-done(((bf16[1,256,2048]{2,1,0:T(8,128)(2,1)}), bf16[1,1024,2048]{2,1,0:T(8,128)(2,1)}) %all-gather.33.cloned.1.call-update) | async-done | bytes 4194320 | tf_op jit(solution)/shard_map/all_gather | solution.py:227
  632.2 102.1 %all-gather.31.cloned.1.call-done = bf16[1536,2048]{1,0:T(8,128)(2,1)} async-done(((bf16[1536,256]{1,0:T(8,128)(2,1)}), bf16[1536,2048]{1,0:T(8,128)(2,1)}) %all-gather.31.cloned.1.call-update) | async-done | bytes 6291472 | tf_op jit(solution)/shard_map/all_gather | solution.py:73
  734.2 16.7 multiply_convert_fusion
  751.0 6.7 fusion.107
  757.7 11.9 add_bitcast_fusion
  769.7 11.1 convert_bitcast_fusion
  780.9 58.8 %reduce-scatter.17.cloned.1.call-done = f32[1,256,2048]{2,1,0:T(8,128)} async-done(((f32[1,1024,2048]{2,1,0:T(8,128)}), f32[1,256,2048]{2,1,0:T(8,128)}) %reduce-scatter.17.cloned.1.call-update) | async-done | bytes 2097168 | tf_op jit(solution)/shard_map/reduce_scatter | solution.py:239
  841.9 44.7 %reduce-scatter.15.cloned.1.call-done = bf16[1,256,2048]{2,1,0:T(8,128)(2,1)} async-done(((bf16[1,1024,2048]{2,1,0:T(8,128)(2,1)}), bf16[1,256,2048]{2,1,0:T(8,128)(2,1)}) %reduce-scatter.15.cloned.1.call-update) | async-done | bytes 1048592 | tf_op jit(solution)/shard_map/reduce_scatter | solution.py:207
  886.6 5.8 fusion.105
  892.4 11.5 convolution_convert_fusion
  904.0 11.5 convolution_convert_fusion.1
  915.6 11.5 convolution_convert_fusion.2
  927.7 7.5 multiply_convert_fusion.3
  935.3 9.4 fusion.90
  947.8 10.8 fusion
  958.9 13.4 fusion.2
  985.1 5.9 fusion.50
  991.1 6.4 fusion.47
  1013.6 5.7 fusion.110
  1019.3 5.6 fusion.108
  1024.9 9.3 fusion.43
  1034.3 15.1 reduce-scatter.35.cloned.1.call-done
  1051.7 118.6 %reduce-scatter.33.cloned.1.call-done = bf16[256,1536]{1,0:T(8,128)(2,1)} async-done(((bf16[2048,1536]{1,0:T(8,128)(2,1)}), bf16[256,1536]{1,0:T(8,128)(2,1)}) %reduce-scatter.33.cloned.1.call-update) | async-done | bytes 786448 | tf_op jit(solution)/shard_map/reduce_scatter | solution.py:248
  1172.8 118.5 %reduce-scatter.31.cloned.1.call-done = bf16[256,1536]{1,0:T(8,128)(2,1)} async-done(((bf16[2048,1536]{1,0:T(8,128)(2,1)}), bf16[256,1536]{1,0:T(8,128)(2,1)}) %reduce-scatter.31.cloned.1.call-update) | async-done | bytes 786448 | tf_op jit(solution)/shard_map/reduce_scatter | solution.py:245
  1293.8 63.9 %reduce-scatter.25.cloned.1.call-done = bf16[256,256]{1,0:T(8,128)(2,1)} async-done(((bf16[2048,256]{1,0:T(8,128)(2,1)}), bf16[256,256]{1,0:T(8,128)(2,1)}) %reduce-scatter.25.cloned.1.call-update) | async-done | bytes 131088 | tf_op jit(solution)/shard_map/reduce_scatter | solution.py:317
  1359.3 64.1 %reduce-scatter.23.cloned.1.call-done = bf16[256,256]{1,0:T(8,128)(2,1)} async-done(((bf16[2048,256]{1,0:T(8,128)(2,1)}), bf16[256,256]{1,0:T(8,128)(2,1)}) %reduce-scatter.23.cloned.1.call-update) | async-done | bytes 131088 | tf_op jit(solution)/shard_map/reduce_scatter | solution.py:314
  1425.1 69.7 %reduce-scatter.29.cloned.1.call-done = bf16[512,256]{1,0:T(8,128)(2,1)} async-done(((bf16[512,2048]{1,0:T(8,128)(2,1)}), bf16[512,256]{1,0:T(8,128)(2,1)}) %reduce-scatter.29.cloned.1.call-update) | async-done | bytes 262160 | tf_op jit(solution)/shard_map/reduce_scatter | solution.py:323
  1496.6 69.0 %reduce-scatter.27.cloned.1.call-done = bf16[256,512]{1,0:T(8,128)(2,1)} async-done(((bf16[2048,512]{1,0:T(8,128)(2,1)}), bf16[256,512]{1,0:T(8,128)(2,1)}) %reduce-scatter.27.cloned.1.call-update) | async-done | bytes 262160 | tf_op jit(solution)/shard_map/reduce_scatter | solution.py:320
  1567.4 69.1 %reduce-scatter.21.cloned.1.call-done = bf16[256,512]{1,0:T(8,128)(2,1)} async-done(((bf16[2048,512]{1,0:T(8,128)(2,1)}), bf16[256,512]{1,0:T(8,128)(2,1)}) %reduce-scatter.21.cloned.1.call-update) | async-done | bytes 262160 | tf_op jit(solution)/shard_map/reduce_scatter | solution.py:311
  1638.3 44.3 %reduce-scatter.19.cloned.1.call-done = bf16[1,256,2048]{2,1,0:T(8,128)(2,1)} async-done(((bf16[1,1024,2048]{2,1,0:T(8,128)(2,1)}), bf16[1,256,2048]{2,1,0:T(8,128)(2,1)}) %reduce-scatter.19.cloned.1.call-update) | async-done | bytes 1048592 | tf_op jit(solution)/shard_map/reduce_scatter | solution.py:295
  1684.4 39.8 %all-reduce = (f32[2048]{0:T(1024)}, f32[128]{0:T(128)}, f32[128]{0:T(128)}, f32[2048]{0:T(1024)}) all-reduce(f32[2048]{0:T(1024)S(1)} %get-tuple-element.57, f32[128]{0:T(128)S(1)} %bitcast_reduce_fusion, f32[128]{0:T(128)S(1)} %bitcast_reduce_fusion.1, f32[2048]{0:T(1024)S(1)} %get-tuple-element.55), channel_id=1, replica_groups=mesh['dp'=8,'ctx'=4] {'dp','ctx'}, use_global_device_ids=true, to_apply=%region_17.18 | all-reduce | flops 4352 | bytes 34816 | tf_op jit(solution)/shard_map/psum | solution.py:327
  (248 shorter events, 98.5 us)
Async XLA Ops:
  7.2 45.9 %all-gather.17.cloned.1.call-start = ((), (), s32[]{:S(2)}) async-start(), calls=%async_computation.14 | async-start | bytes 1179648 | tf_op jit(solution)/shard_map/all_gather | solution.py:62
  7.2 9.9 copy-start.60
  7.2 9.9 copy-start.61
  7.9 80.6 %all-gather.13.cloned.1.call-start = ((), (), s32[]{:S(2)}) async-start(), calls=%async_computation.12 | async-start | bytes 5242880 | tf_op jit(solution)/shard_map/all_gather | solution.py:161
  13.3 126.7 %all-gather.19.cloned.1.call-start = ((), (), s32[]{:S(2)}) async-start(), calls=%async_computation.15 | async-start | bytes 2359296 | tf_op jit(solution)/shard_map/all_gather | solution.py:61
  14.0 166.6 %all-gather.15.cloned.1.call-start = ((), (), s32[]{:S(2)}) async-start(), calls=%async_computation.13 | async-start | bytes 1179648 | tf_op jit(solution)/shard_map/all_gather | solution.py:63
  14.6 216.1 %all-gather.21.cloned.1.call-start = ((), (), s32[]{:S(2)}) async-start(), calls=%async_computation.16 | async-start | bytes 2359296 | tf_op jit(solution)/shard_map/all_gather | solution.py:64
  15.2 267.0 %all-gather.23.cloned.1.call-start = ((), (), s32[]{:S(2)}) async-start(), calls=%async_computation.17 | async-start | bytes 2359296 | tf_op jit(solution)/shard_map/all_gather | solution.py:65
  15.8 343.8 %reduce-scatter.13.cloned.1.call-start = ((), (), s32[]{:S(2)}) async-start(), calls=%async_computation.18 | async-start | bytes 10485760 | tf_op jit(solution)/shard_map/reduce_scatter | solution.py:189
  17.1 128.9 %copy-start.46 = (f32[128]{0:T(128)}, f32[128]{0:T(128)S(1)}, u32[]{:S(2)}) copy-start(f32[128]{0:T(128)S(1)} %convert_element_type.231) | copy-start | bytes 1540
  17.2 135.0 %copy-start.50 = (f32[128]{0:T(128)}, f32[128]{0:T(128)S(1)}, u32[]{:S(2)}) copy-start(f32[128]{0:T(128)S(1)} %convert_element_type.229) | copy-start | bytes 1540
  18.2 74.1 %copy-start.16 = (f32[1024,64]{0,1:T(8,128)}, f32[1024,64]{0,1:T(8,128)S(1)}, u32[]{:S(2)}) copy-start(f32[1024,64]{0,1:T(8,128)S(1)} %get-tuple-element.102) | copy-start | bytes 786436
  18.2 128.3 %copy-start.14 = (f32[1024,64]{0,1:T(8,128)}, f32[1024,64]{0,1:T(8,128)S(1)}, u32[]{:S(2)}) copy-start(f32[1024,64]{0,1:T(8,128)S(1)} %get-tuple-element.101) | copy-start | bytes 786436
  18.4 134.1 %copy-start.10 = (f32[1024,64]{1,0:T(8,128)}, f32[1024,64]{1,0:T(8,128)S(1)}, u32[]{:S(2)}) copy-start(f32[1024,64]{1,0:T(8,128)S(1)} %copy.65) | copy-start | bytes 786436
  18.6 133.9 %copy-start.12 = (f32[1024,64]{1,0:T(8,128)}, f32[1024,64]{1,0:T(8,128)S(1)}, u32[]{:S(2)}) copy-start(f32[1024,64]{1,0:T(8,128)S(1)} %copy.66) | copy-start | bytes 786436
  92.3 52.9 %copy-start.7 = (f32[1024,256]{0,1:T(8,128)}, f32[1024,256]{0,1:T(8,128)S(1)}, u32[]{:S(2)}) copy-start(f32[1024,256]{0,1:T(8,128)S(1)} %fusion.35) | copy-start | bytes 3145732
  92.7 59.4 %copy-start.5 = (f32[1,1024,2,128]{3,1,2,0:T(8,128)}, f32[1,1024,2,128]{3,1,2,0:T(8,128)S(1)}, u32[]{:S(2)}) copy-start(f32[1,1024,2,128]{3,1,2,0:T(8,128)S(1)} %copy.64) | copy-start | bytes 3145732
  93.4 58.8 %copy-start.40 = (f32[1024,2]{0,1:T(2,128)}, f32[1024,2]{0,1:T(2,128)S(1)}, u32[]{:S(2)}) copy-start(f32[1024,2]{0,1:T(2,128)S(1)} %get-tuple-element.100) | copy-start | bytes 24580
  153.0 9.0 copy-start.25
  153.0 9.0 copy-start.27
  200.4 37.2 %copy-start.65 = (f32[2,128,2,1024]{3,1,2,0:T(8,128)}, f32[2,128,2,1024]{3,1,2,0:T(8,128)S(1)}, u32[]{:S(2)}) copy-start(f32[2,128,2,1024]{3,1,2,0:T(8,128)S(1)} %fusion.8) | copy-start | bytes 6291460
  237.5 51.9 %copy-start.63 = (bf16[1024,512]{0,1:T(8,128)(2,1)}, bf16[1024,512]{0,1:T(8,128)(2,1)S(1)}, u32[]{:S(2)}) copy-start(bf16[1024,512]{0,1:T(8,128)(2,1)S(1)} %get-tuple-element.109) | copy-start | bytes 3145732
  289.5 70.1 %copy-start.1 = (bf16[1,256,2048]{2,1,0:T(8,128)(2,1)S(1)}, bf16[1,256,2048]{2,1,0:T(8,128)(2,1)}, u32[]{:S(2)}) copy-start(bf16[1,256,2048]{2,1,0:T(8,128)(2,1)} %param.18) | copy-start | bytes 3145732
  289.5 171.5 %all-gather.29.cloned.1.call-start = ((), (), s32[]{:S(2)}) async-start(), calls=%async_computation.21 | async-start | bytes 7077888 | tf_op jit(solution)/shard_map/all_gather | solution.py:72
  290.2 205.7 %all-gather.25.cloned.1.call-start = ((), (), s32[]{:S(2)}) async-start(), calls=%async_computation.19 | async-start | bytes 5242880 | tf_op jit(solution)/shard_map/all_gather | solution.py:196
  363.1 234.2 %all-gather.27.cloned.1.call-start = ((), (), s32[]{:S(2)}) async-start(), calls=%async_computation.20 | async-start | bytes 7077888 | tf_op jit(solution)/shard_map/all_gather | solution.py:71
  363.7 268.5 %all-gather.33.cloned.1.call-start = ((), (), s32[]{:S(2)}) async-start(), calls=%async_computation.24 | async-start | bytes 5242880 | tf_op jit(solution)/shard_map/all_gather | solution.py:227
  368.1 366.2 %all-gather.31.cloned.1.call-start = ((), (), s32[]{:S(2)}) async-start(), calls=%async_computation.22 | async-start | bytes 7077888 | tf_op jit(solution)/shard_map/all_gather | solution.py:73
  368.6 471.1 %reduce-scatter.17.cloned.1.call-start = ((), (), s32[]{:S(2)}) async-start(), calls=%async_computation.25 | async-start | bytes 10485760 | tf_op jit(solution)/shard_map/reduce_scatter | solution.py:239
  734.2 16.7 copy-start.55
  769.6 117.0 %reduce-scatter.15.cloned.1.call-start = ((), (), s32[]{:S(2)}) async-start(), calls=%async_computation.23 | async-start | bytes 5242880 | tf_op jit(solution)/shard_map/reduce_scatter | solution.py:207
  780.8 146.9 %all-gather.35.cloned.1.call-start = ((), (), s32[]{:S(2)}) async-start(), calls=%async_computation.26 | async-start | bytes 5242880 | tf_op jit(solution)/shard_map/all_gather | solution.py:257
  892.4 157.0 %reduce-scatter.35.cloned.1.call-start = ((), (), s32[]{:S(2)}) async-start(), calls=%async_computation.35 | async-start | bytes 7077888 | tf_op jit(solution)/shard_map/reduce_scatter | solution.py:251
  904.0 266.3 %reduce-scatter.33.cloned.1.call-start = ((), (), s32[]{:S(2)}) async-start(), calls=%async_computation.34 | async-start | bytes 7077888 | tf_op jit(solution)/shard_map/reduce_scatter | solution.py:248
  915.5 375.8 %reduce-scatter.31.cloned.1.call-start = ((), (), s32[]{:S(2)}) async-start(), calls=%async_computation.33 | async-start | bytes 7077888 | tf_op jit(solution)/shard_map/reduce_scatter | solution.py:245
  927.1 430.6 %reduce-scatter.25.cloned.1.call-start = ((), (), s32[]{:S(2)}) async-start(), calls=%async_computation.30 | async-start | bytes 1179648 | tf_op jit(solution)/shard_map/reduce_scatter | solution.py:317
  935.3 10.2 copy-start.56
  958.7 464.8 %reduce-scatter.23.cloned.1.call-start = ((), (), s32[]{:S(2)}) async-start(), calls=%async_computation.29 | async-start | bytes 1179648 | tf_op jit(solution)/shard_map/reduce_scatter | solution.py:314
  958.9 13.4 copy-start.20
  958.9 13.4 copy-start.22
  985.0 509.8 %reduce-scatter.29.cloned.1.call-start = ((), (), s32[]{:S(2)}) async-start(), calls=%async_computation.32 | async-start | bytes 2359296 | tf_op jit(solution)/shard_map/reduce_scatter | solution.py:323
  991.0 574.6 %reduce-scatter.27.cloned.1.call-start = ((), (), s32[]{:S(2)}) async-start(), calls=%async_computation.31 | async-start | bytes 2359296 | tf_op jit(solution)/shard_map/reduce_scatter | solution.py:320
  997.5 639.0 %reduce-scatter.21.cloned.1.call-start = ((), (), s32[]{:S(2)}) async-start(), calls=%async_computation.28 | async-start | bytes 2359296 | tf_op jit(solution)/shard_map/reduce_scatter | solution.py:311
  1011.6 670.9 %reduce-scatter.19.cloned.1.call-start = ((), (), s32[]{:S(2)}) async-start(), calls=%async_computation.27 | async-start | bytes 5242880 | tf_op jit(solution)/shard_map/reduce_scatter | solution.py:295
  1172.8 509.8 %copy-start.39 = (f32[2048]{0:T(1024)S(1)}, f32[2048]{0:T(1024)}, u32[]{:S(2)}) copy-start(f32[2048]{0:T(1024)} %copy-done.38) | copy-start | bytes 24580
  1172.8 509.8 %copy-start.45 = (f32[256]{0:T(256)S(1)}, f32[256]{0:T(256)}, u32[]{:S(2)}) copy-start(f32[256]{0:T(256)} %copy-done.44) | copy-start | bytes 3076
  1293.8 430.4 %copy-start.9 = (f32[1,256,2048]{2,1,0:T(8,128)S(1)}, f32[1,256,2048]{2,1,0:T(8,128)}, u32[]{:S(2)}) copy-start(f32[1,256,2048]{2,1,0:T(8,128)} %get-tuple-element.76) | copy-start | bytes 6291460
  1293.8 430.4 %copy-start.49 = (f32[256]{0:T(256)S(1)}, f32[256]{0:T(256)}, u32[]{:S(2)}) copy-start(f32[256]{0:T(256)} %get-tuple-element.103) | copy-start | bytes 3076
  (43 other events, 144.6 us)
Sparse Core Ops, SparseCore 0:
  10.1 42.9 all-gather.16
  55.2 33.2 all-gather.12
  90.6 49.2 all-gather.18
  141.9 38.6 all-gather.14
  182.6 48.0 all-gather.20
  232.6 49.5 all-gather.22
  289.6 69.8 reduce-scatter.12
  361.9 99.0 all-gather.28
  463.2 32.6 all-gather.24
  498.2 99.0 all-gather.26
  599.5 32.6 all-gather.32
  634.3 99.9 all-gather.30
  769.8 69.9 reduce-scatter.16
  842.1 44.4 reduce-scatter.14
  892.5 34.4 all-gather.34
  930.9 118.3 reduce-scatter.34
  1053.2 117.0 reduce-scatter.32
  1174.2 117.0 reduce-scatter.30
  1295.1 62.5 reduce-scatter.24
  1361.0 62.4 reduce-scatter.22
  1427.4 67.3 reduce-scatter.28
  1498.7 66.7 reduce-scatter.26
  1569.5 66.9 reduce-scatter.20
  1639.0 43.4 reduce-scatter.18
where the time goes:
time: 1740 us; the launch traced here: 1730 us
  waiting for transfers between devices  1360 us (78%)
  matrix products  228 us (13%)
  other arithmetic  73.9 us (4%)
  blocking collectives  39.8 us (2%)
    reduce_scatter x1, waiting for transfers between devices, per_device(): lax.psum_scatter(grad_up.astype(jnp.bfloat16), 'dp', scatter_dimension=0,...  119 us
    reduce_scatter x1, waiting for transfers between devices, per_device(): lax.psum_scatter(grad_gate.astype(jnp.bfloat16), 'dp', scatter_dimension=...  119 us
    all_gather x1, waiting for transfers between devices, swiglu_weights(): lax.all_gather(swiglu_down, 'dp', axis=1, tiled=True)  102 us
    all_gather x1, waiting for transfers between devices, swiglu_weights(): lax.all_gather(swiglu_up, 'dp', axis=0, tiled=True)  92.3 us
    all_gather x1, waiting for transfers between devices, swiglu_weights(): lax.all_gather(swiglu_gate, 'dp', axis=0, tiled=True)  89.6 us
    reduce_scatter x1, waiting for transfers between devices, per_device(): lax.psum_scatter(grad_output.astype(jnp.bfloat16), 'dp', scatter_dimensio...  69.7 us
    reduce_scatter x1, waiting for transfers between devices, per_device(): lax.psum_scatter(branch_part, 'ctx', scatter_dimension=1, tiled=True)  69.2 us
    reduce_scatter x1, waiting for transfers between devices, per_device(): lax.psum_scatter(grad_query.astype(jnp.bfloat16), 'dp', scatter_dimension...  69.1 us
  transfers between devices with their start and end apart: 24, of which 23 were waited for; matrix products, arithmetic and copies ran while one was open for 15% of the time, Pallas kernels for 0%

commit v1 on v0

--- a/solution.py
+++ b/solution.py
@@ -324,9 +324,9 @@
             grad_output.astype(jnp.bfloat16), "dp", scatter_dimension=1, tiled=True
         ).astype(jnp.float32),
     )
-    gain_grads = lax.psum(
-        (grad_gain_in, grad_gain_mid, grad_query_gain, grad_key_gain), ("dp", "ctx")
-    )
+    gain_grads = (grad_gain_in, grad_gain_mid, grad_query_gain, grad_key_gain)
+    for k in ("dp", "ctx"):
+        gain_grads = jax.lax.psum(gain_grads, k)
     return (
         layer_out.reshape(seq_count, local_len, model_width),
         input_grad.reshape(seq_count, local_len, model_width),

time: 1740 us -> 1750 us (level)
    psum x1 -> x2, blocking collectives: 39.8 us -> 48 us  [per_device(): gain_grads = jax.lax.psum(gain_grads, k)]
where the time goes in v1:
time: 1750 us; the launch traced here: 1740 us
  waiting for transfers between devices  1360 us (78%)
  matrix products  228 us (13%)
  other arithmetic  73.9 us (4%)
  blocking collectives  48 us (3%)
    reduce_scatter x1, waiting for transfers between devices, per_device(): lax.psum_scatter(grad_up.astype(jnp.bfloat16), 'dp', scatter_dimension=0,...  119 us
    reduce_scatter x1, waiting for transfers between devices, per_device(): lax.psum_scatter(grad_gate.astype(jnp.bfloat16), 'dp', scatter_dimension=...  119 us
    all_gather x1, waiting for transfers between devices, swiglu_weights(): lax.all_gather(swiglu_down, 'dp', axis=1, tiled=True)  102 us
    all_gather x1, waiting for transfers between devices, swiglu_weights(): lax.all_gather(swiglu_up, 'dp', axis=0, tiled=True)  92.3 us
    all_gather x1, waiting for transfers between devices, swiglu_weights(): lax.all_gather(swiglu_gate, 'dp', axis=0, tiled=True)  89.5 us
    reduce_scatter x1, waiting for transfers between devices, per_device(): lax.psum_scatter(grad_output.astype(jnp.bfloat16), 'dp', scatter_dimensio...  69.7 us
    reduce_scatter x1, waiting for transfers between devices, per_device(): lax.psum_scatter(branch_part, 'ctx', scatter_dimension=1, tiled=True)  69.2 us
    reduce_scatter x1, waiting for transfers between devices, per_device(): lax.psum_scatter(grad_gating.astype(jnp.bfloat16), 'dp', scatter_dimensio...  69.1 us
  transfers between devices with their start and end apart: 24, of which 23 were waited for; matrix products, arithmetic and copies ran while one was open for 15% of the time, Pallas kernels for 0%

profile of v1, /device:TPU:0, one launch (start us, length us, event | category | flops | bytes accessed | tf_op | source)
XLA Modules:
  0.0 1742.8 jit_solution(16299189281773648647)
XLA Ops:
  18.6 34.5 %all-gather.17.cloned.1.call-done = bf16[2048,256]{1,0:T(8,128)(2,1)} async-done(((bf16[256,256]{1,0:T(8,128)(2,1)}), bf16[2048,256]{1,0:T(8,128)(2,1)}) %all-gather.17.cloned.1.call-update) | async-done | bytes 1048592 | tf_op jit(solution)/shard_map/all_gather | solution.py:62
  53.1 35.4 %all-gather.13.cloned.1.call-done = bf16[1,1024,2048]{2,1,0:T(8,128)(2,1)} async-done(((bf16[1,256,2048]{2,1,0:T(8,128)(2,1)}), bf16[1,1024,2048]{2,1,0:T(8,128)(2,1)}) %all-gather.13.cloned.1.call-update) | async-done | bytes 4194320 | tf_op jit(solution)/shard_map/all_gather | solution.py:161
  93.4 46.5 %all-gather.19.cloned.1.call-done = bf16[2048,512]{1,0:T(8,128)(2,1)} async-done(((bf16[256,512]{1,0:T(8,128)(2,1)}), bf16[2048,512]{1,0:T(8,128)(2,1)}) %all-gather.19.cloned.1.call-update) | async-done | bytes 2097168 | tf_op jit(solution)/shard_map/all_gather | solution.py:61
  153.7 8.3 fusion.106
  162.0 18.6 %all-gather.15.cloned.1.call-done = bf16[2048,256]{1,0:T(8,128)(2,1)} async-done(((bf16[256,256]{1,0:T(8,128)(2,1)}), bf16[2048,256]{1,0:T(8,128)(2,1)}) %all-gather.15.cloned.1.call-update) | async-done | bytes 1048592 | tf_op jit(solution)/shard_map/all_gather | solution.py:63
  184.4 8.4 fusion.3
  192.9 7.5 fusion.8
  200.4 30.4 %all-gather.21.cloned.1.call-done = bf16[2048,512]{1,0:T(8,128)(2,1)} async-done(((bf16[256,512]{1,0:T(8,128)(2,1)}), bf16[2048,512]{1,0:T(8,128)(2,1)}) %all-gather.21.cloned.1.call-update) | async-done | bytes 2097168 | tf_op jit(solution)/shard_map/all_gather | solution.py:64
  230.8 6.9 fusion.74
  237.7 44.6 %all-gather.23.cloned.1.call-done = bf16[512,2048]{1,0:T(8,128)(2,1)} async-done(((bf16[512,256]{1,0:T(8,128)(2,1)}), bf16[512,2048]{1,0:T(8,128)(2,1)}) %all-gather.23.cloned.1.call-update) | async-done | bytes 2097168 | tf_op jit(solution)/shard_map/all_gather | solution.py:65
  282.3 7.3 convolution_bitcast_fusion
  290.5 69.2 %reduce-scatter.13.cloned.1.call-done = f32[1,256,2048]{2,1,0:T(8,128)} async-done(((f32[1,1024,2048]{2,1,0:T(8,128)}), f32[1,256,2048]{2,1,0:T(8,128)}) %reduce-scatter.13.cloned.1.call-update) | async-done | bytes 2097168 | tf_op jit(solution)/shard_map/reduce_scatter | solution.py:189
  368.8 92.3 %all-gather.29.cloned.1.call-done = bf16[2048,1536]{1,0:T(8,128)(2,1)} async-done(((bf16[256,1536]{1,0:T(8,128)(2,1)}), bf16[2048,1536]{1,0:T(8,128)(2,1)}) %all-gather.29.cloned.1.call-update) | async-done | bytes 6291472 | tf_op jit(solution)/shard_map/all_gather | solution.py:72
  461.2 34.9 %all-gather.25.cloned.1.call-done = bf16[1,1024,2048]{2,1,0:T(8,128)(2,1)} async-done(((bf16[1,256,2048]{2,1,0:T(8,128)(2,1)}), bf16[1,1024,2048]{2,1,0:T(8,128)(2,1)}) %all-gather.25.cloned.1.call-update) | async-done | bytes 4194320 | tf_op jit(solution)/shard_map/all_gather | solution.py:196
  496.1 11.8 fusion.19
  507.9 89.5 %all-gather.27.cloned.1.call-done = bf16[2048,1536]{1,0:T(8,128)(2,1)} async-done(((bf16[256,1536]{1,0:T(8,128)(2,1)}), bf16[2048,1536]{1,0:T(8,128)(2,1)}) %all-gather.27.cloned.1.call-update) | async-done | bytes 6291472 | tf_op jit(solution)/shard_map/all_gather | solution.py:71
  597.4 11.7 fusion.21
  609.1 23.2 %all-gather.33.cloned.1.call-done = bf16[1,1024,2048]{2,1,0:T(8,128)(2,1)} async-done(((bf16[1,256,2048]{2,1,0:T(8,128)(2,1)}), bf16[1,1024,2048]{2,1,0:T(8,128)(2,1)}) %all-gather.33.cloned.1.call-update) | async-done | bytes 4194320 | tf_op jit(solution)/shard_map/all_gather | solution.py:227
  632.3 102.1 %all-gather.31.cloned.1.call-done = bf16[1536,2048]{1,0:T(8,128)(2,1)} async-done(((bf16[1536,256]{1,0:T(8,128)(2,1)}), bf16[1536,2048]{1,0:T(8,128)(2,1)}) %all-gather.31.cloned.1.call-update) | async-done | bytes 6291472 | tf_op jit(solution)/shard_map/all_gather | solution.py:73
  734.4 16.9 multiply_convert_fusion
  751.3 6.7 fusion.107
  758.0 11.9 add_bitcast_fusion
  770.0 11.1 convert_bitcast_fusion
  781.2 58.8 %reduce-scatter.17.cloned.1.call-done = f32[1,256,2048]{2,1,0:T(8,128)} async-done(((f32[1,1024,2048]{2,1,0:T(8,128)}), f32[1,256,2048]{2,1,0:T(8,128)}) %reduce-scatter.17.cloned.1.call-update) | async-done | bytes 2097168 | tf_op jit(solution)/shard_map/reduce_scatter | solution.py:239
  842.2 44.7 %reduce-scatter.15.cloned.1.call-done = bf16[1,256,2048]{2,1,0:T(8,128)(2,1)} async-done(((bf16[1,1024,2048]{2,1,0:T(8,128)(2,1)}), bf16[1,256,2048]{2,1,0:T(8,128)(2,1)}) %reduce-scatter.15.cloned.1.call-update) | async-done | bytes 1048592 | tf_op jit(solution)/shard_map/reduce_scatter | solution.py:207
  886.9 5.8 fusion.105
  892.7 11.5 convolution_convert_fusion
  904.3 11.5 convolution_convert_fusion.1
  915.9 11.4 convolution_convert_fusion.2
  928.1 7.5 multiply_convert_fusion.3
  935.6 9.4 fusion.90
  948.2 10.8 fusion
  959.5 13.4 fusion.2
  985.6 6.0 fusion.50
  991.7 6.4 fusion.47
  1014.2 5.7 fusion.110
  1025.5 9.3 fusion.43
  1034.8 14.8 reduce-scatter.35.cloned.1.call-done
  1052.0 118.6 %reduce-scatter.33.cloned.1.call-done = bf16[256,1536]{1,0:T(8,128)(2,1)} async-done(((bf16[2048,1536]{1,0:T(8,128)(2,1)}), bf16[256,1536]{1,0:T(8,128)(2,1)}) %reduce-scatter.33.cloned.1.call-update) | async-done | bytes 786448 | tf_op jit(solution)/shard_map/reduce_scatter | solution.py:248
  1173.1 118.6 %reduce-scatter.31.cloned.1.call-done = bf16[256,1536]{1,0:T(8,128)(2,1)} async-done(((bf16[2048,1536]{1,0:T(8,128)(2,1)}), bf16[256,1536]{1,0:T(8,128)(2,1)}) %reduce-scatter.31.cloned.1.call-update) | async-done | bytes 786448 | tf_op jit(solution)/shard_map/reduce_scatter | solution.py:245
  1294.2 64.0 %reduce-scatter.25.cloned.1.call-done = bf16[256,256]{1,0:T(8,128)(2,1)} async-done(((bf16[2048,256]{1,0:T(8,128)(2,1)}), bf16[256,256]{1,0:T(8,128)(2,1)}) %reduce-scatter.25.cloned.1.call-update) | async-done | bytes 131088 | tf_op jit(solution)/shard_map/reduce_scatter | solution.py:317
  1359.8 64.1 %reduce-scatter.23.cloned.1.call-done = bf16[256,256]{1,0:T(8,128)(2,1)} async-done(((bf16[2048,256]{1,0:T(8,128)(2,1)}), bf16[256,256]{1,0:T(8,128)(2,1)}) %reduce-scatter.23.cloned.1.call-update) | async-done | bytes 131088 | tf_op jit(solution)/shard_map/reduce_scatter | solution.py:314
  1425.5 69.7 %reduce-scatter.29.cloned.1.call-done = bf16[512,256]{1,0:T(8,128)(2,1)} async-done(((bf16[512,2048]{1,0:T(8,128)(2,1)}), bf16[512,256]{1,0:T(8,128)(2,1)}) %reduce-scatter.29.cloned.1.call-update) | async-done | bytes 262160 | tf_op jit(solution)/shard_map/reduce_scatter | solution.py:323
  1497.0 69.1 %reduce-scatter.27.cloned.1.call-done = bf16[256,512]{1,0:T(8,128)(2,1)} async-done(((bf16[2048,512]{1,0:T(8,128)(2,1)}), bf16[256,512]{1,0:T(8,128)(2,1)}) %reduce-scatter.27.cloned.1.call-update) | async-done | bytes 262160 | tf_op jit(solution)/shard_map/reduce_scatter | solution.py:320
  1567.9 69.1 %reduce-scatter.21.cloned.1.call-done = bf16[256,512]{1,0:T(8,128)(2,1)} async-done(((bf16[2048,512]{1,0:T(8,128)(2,1)}), bf16[256,512]{1,0:T(8,128)(2,1)}) %reduce-scatter.21.cloned.1.call-update) | async-done | bytes 262160 | tf_op jit(solution)/shard_map/reduce_scatter | solution.py:311
  1638.8 44.2 %reduce-scatter.19.cloned.1.call-done = bf16[1,256,2048]{2,1,0:T(8,128)(2,1)} async-done(((bf16[1,1024,2048]{2,1,0:T(8,128)(2,1)}), bf16[1,256,2048]{2,1,0:T(8,128)(2,1)}) %reduce-scatter.19.cloned.1.call-update) | async-done | bytes 1048592 | tf_op jit(solution)/shard_map/reduce_scatter | solution.py:295
  1684.9 37.1 %all-reduce = (f32[2048]{0:T(1024)S(1)}, f32[128]{0:T(128)S(1)}, f32[128]{0:T(128)S(1)}, f32[2048]{0:T(1024)S(1)}) all-reduce(f32[2048]{0:T(1024)S(1)} %get-tuple-element.57, f32[128]{0:T(128)S(1)} %bitcast_reduce_fusion, f32[128]{0:T(128)S(1)} %bitcast_reduce_fusion.1, ...), channel_id=1, replica_groups=mesh['dp'=8,'ctx'=4] {'dp'}, use_global_device_ids=true, to_apply=%region_17.18 | all-reduce | flops 4352 | bytes 34816 | tf_op jit(solution)/shard_map/psum | solution.py:329
  1722.0 10.9 all-reduce.1
  (249 shorter events, 104.4 us)
Async XLA Ops:
  7.2 45.9 %all-gather.17.cloned.1.call-start = ((), (), s32[]{:S(2)}) async-start(), calls=%async_computation.14 | async-start | bytes 1179648 | tf_op jit(solution)/shard_map/all_gather | solution.py:62
  7.2 9.9 copy-start.60
  7.2 9.9 copy-start.61
  7.9 80.6 %all-gather.13.cloned.1.call-start = ((), (), s32[]{:S(2)}) async-start(), calls=%async_computation.12 | async-start | bytes 5242880 | tf_op jit(solution)/shard_map/all_gather | solution.py:161
  13.3 126.7 %all-gather.19.cloned.1.call-start = ((), (), s32[]{:S(2)}) async-start(), calls=%async_computation.15 | async-start | bytes 2359296 | tf_op jit(solution)/shard_map/all_gather | solution.py:61
  14.0 166.6 %all-gather.15.cloned.1.call-start = ((), (), s32[]{:S(2)}) async-start(), calls=%async_computation.13 | async-start | bytes 1179648 | tf_op jit(solution)/shard_map/all_gather | solution.py:63
  14.6 216.2 %all-gather.21.cloned.1.call-start = ((), (), s32[]{:S(2)}) async-start(), calls=%async_computation.16 | async-start | bytes 2359296 | tf_op jit(solution)/shard_map/all_gather | solution.py:64
  15.2 267.1 %all-gather.23.cloned.1.call-start = ((), (), s32[]{:S(2)}) async-start(), calls=%async_computation.17 | async-start | bytes 2359296 | tf_op jit(solution)/shard_map/all_gather | solution.py:65
  15.8 343.9 %reduce-scatter.13.cloned.1.call-start = ((), (), s32[]{:S(2)}) async-start(), calls=%async_computation.18 | async-start | bytes 10485760 | tf_op jit(solution)/shard_map/reduce_scatter | solution.py:189
  17.1 128.9 %copy-start.46 = (f32[128]{0:T(128)}, f32[128]{0:T(128)S(1)}, u32[]{:S(2)}) copy-start(f32[128]{0:T(128)S(1)} %convert_element_type.231) | copy-start | bytes 1540
  17.2 135.0 %copy-start.50 = (f32[128]{0:T(128)}, f32[128]{0:T(128)S(1)}, u32[]{:S(2)}) copy-start(f32[128]{0:T(128)S(1)} %convert_element_type.229) | copy-start | bytes 1540
  18.2 74.1 %copy-start.16 = (f32[1024,64]{0,1:T(8,128)}, f32[1024,64]{0,1:T(8,128)S(1)}, u32[]{:S(2)}) copy-start(f32[1024,64]{0,1:T(8,128)S(1)} %get-tuple-element.106) | copy-start | bytes 786436
  18.2 128.4 %copy-start.14 = (f32[1024,64]{0,1:T(8,128)}, f32[1024,64]{0,1:T(8,128)S(1)}, u32[]{:S(2)}) copy-start(f32[1024,64]{0,1:T(8,128)S(1)} %get-tuple-element.105) | copy-start | bytes 786436
  18.4 134.2 %copy-start.10 = (f32[1024,64]{1,0:T(8,128)}, f32[1024,64]{1,0:T(8,128)S(1)}, u32[]{:S(2)}) copy-start(f32[1024,64]{1,0:T(8,128)S(1)} %copy.65) | copy-start | bytes 786436
  18.6 133.9 %copy-start.12 = (f32[1024,64]{1,0:T(8,128)}, f32[1024,64]{1,0:T(8,128)S(1)}, u32[]{:S(2)}) copy-start(f32[1024,64]{1,0:T(8,128)S(1)} %copy.66) | copy-start | bytes 786436
  92.3 52.9 %copy-start.7 = (f32[1024,256]{0,1:T(8,128)}, f32[1024,256]{0,1:T(8,128)S(1)}, u32[]{:S(2)}) copy-start(f32[1024,256]{0,1:T(8,128)S(1)} %fusion.35) | copy-start | bytes 3145732
  92.7 59.4 %copy-start.5 = (f32[1,1024,2,128]{3,1,2,0:T(8,128)}, f32[1,1024,2,128]{3,1,2,0:T(8,128)S(1)}, u32[]{:S(2)}) copy-start(f32[1,1024,2,128]{3,1,2,0:T(8,128)S(1)} %copy.64) | copy-start | bytes 3145732
  93.4 58.8 %copy-start.40 = (f32[1024,2]{0,1:T(2,128)}, f32[1024,2]{0,1:T(2,128)S(1)}, u32[]{:S(2)}) copy-start(f32[1024,2]{0,1:T(2,128)S(1)} %get-tuple-element.104) | copy-start | bytes 24580
  153.0 9.0 copy-start.25
  153.0 9.0 copy-start.27
  200.4 37.3 %copy-start.65 = (f32[2,128,2,1024]{3,1,2,0:T(8,128)}, f32[2,128,2,1024]{3,1,2,0:T(8,128)S(1)}, u32[]{:S(2)}) copy-start(f32[2,128,2,1024]{3,1,2,0:T(8,128)S(1)} %fusion.8) | copy-start | bytes 6291460
  237.7 51.9 %copy-start.63 = (bf16[1024,512]{0,1:T(8,128)(2,1)}, bf16[1024,512]{0,1:T(8,128)(2,1)S(1)}, u32[]{:S(2)}) copy-start(bf16[1024,512]{0,1:T(8,128)(2,1)S(1)} %get-tuple-element.113) | copy-start | bytes 3145732
  289.6 70.1 %copy-start.1 = (bf16[1,256,2048]{2,1,0:T(8,128)(2,1)S(1)}, bf16[1,256,2048]{2,1,0:T(8,128)(2,1)}, u32[]{:S(2)}) copy-start(bf16[1,256,2048]{2,1,0:T(8,128)(2,1)} %param.18) | copy-start | bytes 3145732
  289.6 171.5 %all-gather.29.cloned.1.call-start = ((), (), s32[]{:S(2)}) async-start(), calls=%async_computation.21 | async-start | bytes 7077888 | tf_op jit(solution)/shard_map/all_gather | solution.py:72
  290.4 205.7 %all-gather.25.cloned.1.call-start = ((), (), s32[]{:S(2)}) async-start(), calls=%async_computation.19 | async-start | bytes 5242880 | tf_op jit(solution)/shard_map/all_gather | solution.py:196
  363.2 234.2 %all-gather.27.cloned.1.call-start = ((), (), s32[]{:S(2)}) async-start(), calls=%async_computation.20 | async-start | bytes 7077888 | tf_op jit(solution)/shard_map/all_gather | solution.py:71
  363.8 268.5 %all-gather.33.cloned.1.call-start = ((), (), s32[]{:S(2)}) async-start(), calls=%async_computation.24 | async-start | bytes 5242880 | tf_op jit(solution)/shard_map/all_gather | solution.py:227
  368.2 366.2 %all-gather.31.cloned.1.call-start = ((), (), s32[]{:S(2)}) async-start(), calls=%async_computation.22 | async-start | bytes 7077888 | tf_op jit(solution)/shard_map/all_gather | solution.py:73
  368.8 471.2 %reduce-scatter.17.cloned.1.call-start = ((), (), s32[]{:S(2)}) async-start(), calls=%async_computation.25 | async-start | bytes 10485760 | tf_op jit(solution)/shard_map/reduce_scatter | solution.py:239
  734.4 16.9 copy-start.55
  769.9 117.0 %reduce-scatter.15.cloned.1.call-start = ((), (), s32[]{:S(2)}) async-start(), calls=%async_computation.23 | async-start | bytes 5242880 | tf_op jit(solution)/shard_map/reduce_scatter | solution.py:207
  781.1 146.9 %all-gather.35.cloned.1.call-start = ((), (), s32[]{:S(2)}) async-start(), calls=%async_computation.26 | async-start | bytes 5242880 | tf_op jit(solution)/shard_map/all_gather | solution.py:257
  892.7 157.0 %reduce-scatter.35.cloned.1.call-start = ((), (), s32[]{:S(2)}) async-start(), calls=%async_computation.35 | async-start | bytes 7077888 | tf_op jit(solution)/shard_map/reduce_scatter | solution.py:251
  904.3 266.4 %reduce-scatter.33.cloned.1.call-start = ((), (), s32[]{:S(2)}) async-start(), calls=%async_computation.34 | async-start | bytes 7077888 | tf_op jit(solution)/shard_map/reduce_scatter | solution.py:248
  915.9 375.8 %reduce-scatter.31.cloned.1.call-start = ((), (), s32[]{:S(2)}) async-start(), calls=%async_computation.33 | async-start | bytes 7077888 | tf_op jit(solution)/shard_map/reduce_scatter | solution.py:245
  927.4 430.8 %reduce-scatter.25.cloned.1.call-start = ((), (), s32[]{:S(2)}) async-start(), calls=%async_computation.30 | async-start | bytes 1179648 | tf_op jit(solution)/shard_map/reduce_scatter | solution.py:317
  935.6 10.2 copy-start.56
  959.0 464.8 %reduce-scatter.23.cloned.1.call-start = ((), (), s32[]{:S(2)}) async-start(), calls=%async_computation.29 | async-start | bytes 1179648 | tf_op jit(solution)/shard_map/reduce_scatter | solution.py:314
  959.5 13.4 copy-start.20
  959.5 13.4 copy-start.22
  985.6 509.6 %reduce-scatter.29.cloned.1.call-start = ((), (), s32[]{:S(2)}) async-start(), calls=%async_computation.32 | async-start | bytes 2359296 | tf_op jit(solution)/shard_map/reduce_scatter | solution.py:323
  991.6 574.5 %reduce-scatter.27.cloned.1.call-start = ((), (), s32[]{:S(2)}) async-start(), calls=%async_computation.31 | async-start | bytes 2359296 | tf_op jit(solution)/shard_map/reduce_scatter | solution.py:320
  998.2 638.8 %reduce-scatter.21.cloned.1.call-start = ((), (), s32[]{:S(2)}) async-start(), calls=%async_computation.28 | async-start | bytes 2359296 | tf_op jit(solution)/shard_map/reduce_scatter | solution.py:311
  1012.2 670.8 %reduce-scatter.19.cloned.1.call-start = ((), (), s32[]{:S(2)}) async-start(), calls=%async_computation.27 | async-start | bytes 5242880 | tf_op jit(solution)/shard_map/reduce_scatter | solution.py:295
  1173.1 509.9 %copy-start.39 = (f32[2048]{0:T(1024)S(1)}, f32[2048]{0:T(1024)}, u32[]{:S(2)}) copy-start(f32[2048]{0:T(1024)} %copy-done.38) | copy-start | bytes 24580
  1173.1 509.9 %copy-start.45 = (f32[256]{0:T(256)S(1)}, f32[256]{0:T(256)}, u32[]{:S(2)}) copy-start(f32[256]{0:T(256)} %copy-done.44) | copy-start | bytes 3076
  1294.1 438.8 %copy-start.9 = (f32[1,256,2048]{2,1,0:T(8,128)S(1)}, f32[1,256,2048]{2,1,0:T(8,128)}, u32[]{:S(2)}) copy-start(f32[1,256,2048]{2,1,0:T(8,128)} %get-tuple-element.80) | copy-start | bytes 6291460
  1294.2 438.8 %copy-start.49 = (f32[256]{0:T(256)S(1)}, f32[256]{0:T(256)}, u32[]{:S(2)}) copy-start(f32[256]{0:T(256)} %get-tuple-element.107) | copy-start | bytes 3076
  (43 other events, 144.5 us)
Sparse Core Ops, SparseCore 0:
  10.1 42.9 all-gather.16
  55.2 33.2 all-gather.12
  90.6 49.2 all-gather.18
  141.9 38.6 all-gather.14
  182.6 48.1 all-gather.20
  232.7 49.5 all-gather.22
  289.8 69.8 reduce-scatter.12
  362.1 99.0 all-gather.28
  463.4 32.6 all-gather.24
  498.3 99.0 all-gather.26
  599.6 32.6 all-gather.32
  634.4 99.9 all-gather.30
  770.0 69.9 reduce-scatter.16
  842.4 44.4 reduce-scatter.14
  892.8 34.4 all-gather.34
  931.2 118.3 reduce-scatter.34
  1053.5 117.1 reduce-scatter.32
  1174.5 117.1 reduce-scatter.30
  1295.5 62.6 reduce-scatter.24
  1361.4 62.4 reduce-scatter.22
  1427.8 67.3 reduce-scatter.28
  1499.2 66.9 reduce-scatter.26
  1570.1 66.8 reduce-scatter.20
  1639.6 43.4 reduce-scatter.18
